TPU v7x, 256 devices: a whole 4x4x8 slice. The times are simulated.
256 devices in a mesh: seq: 256 (over y, x, z, core).
Axes of the slice: x: 4, y: 4, z: 8, core: 2. Of those that a mesh axis runs over, the one named last changes fastest.
Arguments:
- queries: bfloat16 [98304, 1024], P('seq'), may hold values from -125 to 125, as said below
- keys_values: bfloat16 [2, 98304, 1024], P(None, 'seq'), may hold values from -6 to 6, as said below
- rand_blocks: int32 [768, 3], P('seq'), may hold values from 0 to 47, as said below
- global_ids: int32 [2], replicated, may hold values from 0 to 767
- out_weight: bfloat16 [1024, 2048], replicated, may hold values from -0.1875 to 0.1875
Outputs:
- layer_out: bfloat16 [98304, 2048], P('seq')
Inputs may be any that keep to these rules, and one draw needn't show every extreme that they name: queries stay within the range. `keys_values`: keys and values stay within the range. `rand_blocks`: entry e names the block held by the segment's device number e // 3. Among the 9 entries of the rows of one device (aligned blocks of 3 rows), no segment device is named more than 1 times, and some segment device is named exactly 1 times.
All inputs are finite; a program needn't handle non-finite values.
Results may differ from a plain program's by a relative error of at most 0.0057.
Values may be sent and summed in bfloat16 or wider, within the bound.
A program may use at most 192 MiB of HBM per device.

v0:
```python
import math

import jax
import jax.numpy as jnp
from jax import lax
from jax.sharding import PartitionSpec as P

HEADS = 8
HEAD_DIM = 128
BLOCK = 128
RAND = 3
GLOB = 2
SEG_DEV = 16


def padded_2(block, sides, width):
    for axis, dim in sides:
        count = lax.axis_size(axis)
        forward = [(i, i + 1) for i in range(count - 1)]
        forward.append((count - 1, 0))
        backward = [(target, source) for source, target in forward]
        low = lax.ppermute(
            lax.slice_in_dim(block, block.shape[dim] - width, None, axis=dim), axis, forward
        )
        high = lax.ppermute(lax.slice_in_dim(block, 0, width, axis=dim), axis, backward)
        block = jnp.concatenate([low, block, high], axis=dim)
    return block


def partner(value, axis, apart):
    mask = 2**apart
    pairs = [(source, source ^ mask) for source in range(lax.axis_size(axis))]
    return lax.ppermute(value, axis, pairs)


def local(queries, keys_values, rand_blocks, global_ids, out_weight):
    tok_rows = queries.shape[0]
    inner_width = queries.shape[1]
    blocks_here = tok_rows // BLOCK
    device = lax.axis_index("seq")
    scale_factor = 1.0 / math.sqrt(HEAD_DIM)
    padded = padded_2(keys_values, (("seq", 1),), BLOCK)
    padded_blocks = padded.reshape(2, blocks_here + 2, BLOCK, inner_width)
    window_keys = jnp.stack(
        [
            padded_blocks[:, 0:blocks_here],
            padded_blocks[:, 1 : blocks_here + 1],
            padded_blocks[:, 2 : blocks_here + 2],
        ],
        axis=2,
    )
    own_pieces = []
    for which_global in range(GLOB):
        local_start = global_ids[which_global] % blocks_here * BLOCK
        own_pieces.append(lax.dynamic_slice_in_dim(keys_values, local_start, BLOCK, 1))
    stacked = jnp.stack(own_pieces, axis=1)
    owned = (global_ids // blocks_here == device).reshape(1, GLOB, 1, 1)
    masked_terms = jnp.where(owned, stacked.astype(jnp.float32), 0.0)
    global_keys = lax.psum(masked_terms, "seq").astype(jnp.bfloat16)
    gathered = keys_values
    for bit_index in range(SEG_DEV.bit_length() - 1):
        partner_part = partner(gathered, "seq", bit_index)
        lower_half = device // 2**bit_index % 2 == 0
        gathered = jnp.where(
            lower_half,
            jnp.concatenate([gathered, partner_part], axis=1),
            jnp.concatenate([partner_part, gathered], axis=1),
        )
    segment_blocks = gathered.reshape(2, SEG_DEV * blocks_here, BLOCK, inner_width)
    random_keys = jnp.take(segment_blocks, rand_blocks.reshape(-1), axis=1)
    random_keys = random_keys.reshape(2, blocks_here, RAND, BLOCK, inner_width)
    global_wide = jnp.broadcast_to(global_keys[:, None], (2, blocks_here, GLOB, BLOCK, inner_width))
    all_keys = jnp.concatenate([window_keys, global_wide, random_keys], axis=2)
    all_keys = all_keys.reshape(2, blocks_here, 8 * BLOCK, HEADS, HEAD_DIM)
    query_blocks = queries.reshape(blocks_here, BLOCK, HEADS, HEAD_DIM)
    scores = (
        jnp.einsum("nqhd,nkhd->nhqk", query_blocks, all_keys[0], preferred_element_type=jnp.float32)
        * scale_factor
    )
    probs = jax.nn.softmax(scores, axis=-1).astype(jnp.bfloat16)
    attended = jnp.einsum("nhqk,nkhd->nqhd", probs, all_keys[1], preferred_element_type=jnp.float32)
    attended = attended.astype(jnp.bfloat16).reshape(tok_rows, inner_width)
    return jnp.dot(attended, out_weight, preferred_element_type=jnp.float32).astype(jnp.bfloat16)


def solution(mesh):
    placed = (P("seq", None), P(None, "seq", None), P("seq", None), P(), P())
    return jax.shard_map(
        local, mesh=mesh, in_specs=placed, out_specs=P("seq", None), check_vma=False
    )
```

profile of v0, /device:TPU:1, one launch (start us, length us, event | category | flops | bytes accessed | tf_op | source)
XLA Modules:
  0.0 1080.2 jit_solution(3509159315627211723)
XLA Ops:
  0.0 3.2 collective-permute-start.2
  3.2 3.4 collective-permute-done.2
  6.6 4.4 maximum_select_fusion.3
  11.0 0.1 collective-permute-start.3
  11.1 69.4 %collective-permute-done.3 = bf16[2,768,1024]{2,1,0:T(8,128)(2,1)} collective-permute-done((bf16[2,768,1024]{2,1,0:T(8,128)(2,1)S(1)}, bf16[2,768,1024]{2,1,0:T(8,128)(2,1)}, u32[]{:S(2)}, u32[]{:S(2)}) %collective-permute-start.3) | collective-permute-done | bytes 3145760 | tf_op jit(solution)/shard_map/ppermute | solution.py:33
  80.5 7.2 maximum_select_fusion.2
  87.6 1.6 collective-permute-start.4
  89.3 0.0 copy-start.3
  89.3 0.0 copy-start
  89.3 0.0 copy-start.2
  89.3 271.6 %collective-permute-done.4 = bf16[2,1536,1024]{2,1,0:T(8,128)(2,1)} collective-permute-done((bf16[2,1536,1024]{2,1,0:T(8,128)(2,1)}, bf16[2,1536,1024]{2,1,0:T(8,128)(2,1)}, u32[]{:S(2)}, u32[]{:S(2)}) %collective-permute-start.4) | collective-permute-done | bytes 6291488 | tf_op jit(solution)/shard_map/ppermute | solution.py:33
  360.9 15.3 %maximum_select_fusion.1 = bf16[2,3072,1024]{2,1,0:T(8,128)(2,1)} fusion(bf16[2,1536,1024]{2,1,0:T(8,128)(2,1)} %collective-permute-done.4, bf16[2,1536,1024]{2,1,0:T(8,128)(2,1)} %maximum_select_fusion.2, pred[]{:T(512)S(6)} %eq.28), kind=kLoop, calls=%fused_computation.3 | loop fusion | flops 56623104 | bytes 25165824 | tf_op jit(solution)/shard_map/jit(_where)/select_n | solution.py:64
  376.2 0.0 copy-start.1
  376.2 4.9 collective-permute-start.5
  381.1 0.0 copy-done.3
  381.1 0.6 fusion.34
  383.0 0.0 copy-done
  383.0 1.2 dynamic-slice_bitcast_fusion.1
  384.2 0.0 collective-permute-start
  384.3 1.3 collective-permute-start.1
  385.5 0.0 copy-done.2
  385.6 0.1 reshape.69
  385.6 1.7 convert_select_fusion
  387.4 0.0 copy-done.1
  387.4 1.1 copy.33
  388.5 588.0 %all-reduce.1 = bf16[2,2,128,1024]{3,2,1,0:T(8,128)(2,1)S(1)} all-reduce(f32[2,2,128,1024]{3,2,1,0:T(8,128)} %convert_select_fusion), channel_id=1, replica_groups=mesh['seq'=256] {'seq'}, use_global_device_ids=true, to_apply=%region_0.1 | all-reduce | flops 524288 | bytes 3145728 | tf_op jit(solution)/shard_map/psum | solution.py:59
  976.5 0.0 collective-permute-done
  976.5 0.0 collective-permute-done.1
  976.5 1.5 pad_maximum_fusion
  978.0 1.3 fusion.13
  979.3 1.4 fusion.12
  980.7 1.3 fusion.11
  982.0 2.1 broadcast_dynamic-update-slice_fusion
  984.1 0.0 collective-permute-done.5
  984.1 26.4 %maximum_select_fusion = bf16[2,6144,1024]{2,1,0:T(8,128)(2,1)} fusion(bf16[2,3072,1024]{2,1,0:T(8,128)(2,1)} %collective-permute-done.5, bf16[2,3072,1024]{2,1,0:T(8,128)(2,1)} %maximum_select_fusion.1, pred[]{:T(512)S(6)} %eq.27), kind=kLoop, calls=%fused_computation.2 | loop fusion | flops 113246208 | bytes 50331648 | tf_op jit(solution)/shard_map/jit(_where)/select_n | solution.py:64
  1010.5 11.8 %gather_fusion = bf16[9,2,128,1024]{3,2,1,0:T(8,128)(2,1)} fusion(bf16[2,48,128,1024]{3,2,1,0:T(8,128)(2,1)} %bitcast.70, s32[1024]{0:T(1024)S(1)} %pad_clamp_fusion), kind=kCustom, calls=%fused_computation | custom fusion | bytes 9437220 | tf_op jit(solution)/shard_map/jit(_take)/gather | solution.py:70
  1022.3 2.8 copy.20
  1025.1 4.0 select_dynamic-update-slice_fusion
  1029.2 5.5 fusion.33
  1034.7 1.6 copy.32
  1036.4 6.8 fusion.8
  1043.1 11.1 %fusion.35 = f32[3,8,128]{2,1,0:T(8,128)S(1)} fusion(f32[3,8,1024,128]{3,2,1,0:T(8,128)} %fusion.8), kind=kOutput, calls=%fused_computation.47 | output fusion | flops 12583935 | bytes 12595200 | tf_op jit(solution)/shard_map/sub | solution.py:80
  1054.2 4.2 copy.31
  1058.5 16.1 %fusion.17 = bf16[3,128,8,128]{1,3,2,0:T(8,128)(2,1)S(1)} fusion(f32[3,8,128]{2,1,0:T(8,128)S(1)} %fusion.35, bf16[3,1024,8,128]{3,2,1,0:T(8,128)(2,1)} %bitcast.79, f32[3,8,1024,128]{3,2,1,0:T(8,128)} %fusion.8), kind=kOutput, calls=%fused_computation.29 | convolution fusion | flops 821432320 | bytes 19673088 | tf_op jit(solution)/shard_map/nhqk,nkhd->nqhd/dot_general | solution.py:81
  1074.6 0.4 copy.28
  1075.0 5.1 convolution_convert_fusion
  (4 shorter events, 0.0 us)
Async XLA Ops:
  0.0 6.6 collective-permute-start.2
  11.0 69.5 %collective-permute-start.3 = (bf16[2,768,1024]{2,1,0:T(8,128)(2,1)S(1)}, bf16[2,768,1024]{2,1,0:T(8,128)(2,1)}, u32[]{:S(2)}, u32[]{:S(2)}) collective-permute-start(bf16[2,768,1024]{2,1,0:T(8,128)(2,1)S(1)} %maximum_select_fusion.3), channel_id=1, source_target_pairs={{0,2},{1,3},{2,0},{3,1},{4,6},{5,7},{6,4},{7,5},{8,10},{9,11},{10,... | collective-permute-start | bytes 9437192 | tf_op jit(solution)/shard_map/ppermute | solution.py:33
  87.6 273.2 %collective-permute-start.4 = (bf16[2,1536,1024]{2,1,0:T(8,128)(2,1)}, bf16[2,1536,1024]{2,1,0:T(8,128)(2,1)}, u32[]{:S(2)}, u32[]{:S(2)}) collective-permute-start(bf16[2,1536,1024]{2,1,0:T(8,128)(2,1)} %maximum_select_fusion.2), channel_id=1, source_target_pairs={{0,4},{1,5},{2,6},{3,7},{4,0},{5,1},{6,2},{7,3},{8,12},{9,13},{10,... | collective-permute-start | bytes 18874376 | tf_op jit(solution)/shard_map/ppermute | solution.py:33
  89.3 291.8 %copy-start.3 = (s32[2]{0:T(128)S(1)}, s32[2]{0:T(128)}, u32[]{:S(2)}) copy-start(s32[2]{0:T(128)} %param.8) | copy-start | bytes 28
  89.3 293.7 %copy-start = (bf16[2,384,1024]{2,1,0:T(8,128)(2,1)S(1)}, bf16[2,384,1024]{2,1,0:T(8,128)(2,1)}, u32[]{:S(2)}) copy-start(bf16[2,384,1024]{2,1,0:T(8,128)(2,1)} %param.6) | copy-start | bytes 4718596
  89.3 296.3 %copy-start.2 = (s32[3,3]{1,0:T(4,128)S(1)}, s32[3,3]{1,0:T(4,128)}, u32[]{:S(2)}) copy-start(s32[3,3]{1,0:T(4,128)} %param.7) | copy-start | bytes 112
  376.2 11.2 %copy-start.1 = (bf16[384,1024]{1,0:T(8,128)(2,1)S(1)}, bf16[384,1024]{1,0:T(8,128)(2,1)}, u32[]{:S(2)}) copy-start(bf16[384,1024]{1,0:T(8,128)(2,1)} %param.5) | copy-start | bytes 2359300
  376.2 607.9 %collective-permute-start.5 = (bf16[2,3072,1024]{2,1,0:T(8,128)(2,1)}, bf16[2,3072,1024]{2,1,0:T(8,128)(2,1)}, u32[]{:S(2)}, u32[]{:S(2)}) collective-permute-start(bf16[2,3072,1024]{2,1,0:T(8,128)(2,1)} %maximum_select_fusion.1), channel_id=1, source_target_pairs={{0,8},{1,9},{2,10},{3,11},{4,12},{5,13},{6,14},{7,15},{8,0},{9,1},... | collective-permute-start | bytes 37748744 | tf_op jit(solution)/shard_map/ppermute | solution.py:33
  384.2 592.2 %collective-permute-start = (bf16[2,128,1024]{2,1,0:T(8,128)(2,1)}, bf16[2,128,1024]{2,1,0:T(8,128)(2,1)}, u32[]{:S(2)}, u32[]{:S(2)}) collective-permute-start(bf16[2,128,1024]{2,1,0:T(8,128)(2,1)} %get-tuple-element.10), channel_id=1, source_target_pairs={{0,1},{1,2},{2,3},{3,4},{4,5},{5,6},{6,7},{7,8},{8,9},{9,10},{10,1... | collective-permute-start | bytes 1572872 | tf_op jit(solution)/shard_map/ppermute | solution.py:22
  384.3 592.2 %collective-permute-start.1 = (bf16[2,128,1024]{2,1,0:T(8,128)(2,1)}, bf16[2,128,1024]{2,1,0:T(8,128)(2,1)}, u32[]{:S(2)}, u32[]{:S(2)}) collective-permute-start(bf16[2,128,1024]{2,1,0:T(8,128)(2,1)} %get-tuple-element.9), channel_id=1, source_target_pairs={{1,0},{2,1},{3,2},{4,3},{5,4},{6,5},{7,6},{8,7},{9,8},{10,9},{11,1... | collective-permute-start | bytes 1572872 | tf_op jit(solution)/shard_map/ppermute | solution.py:25
where the time goes:
time: 1080 us
  blocking collectives  588 us (54%)
  waiting for transfers between devices  344 us (32%)
  other arithmetic  71.6 us (7%)
  local copies, waits for them, and re-layouts  35.6 us (3%)
  matrix products  28 us (3%)
  starting transfers between devices  11.2 us (1%)
    psum x1, blocking collectives, local(): global_keys = lax.psum(masked_terms, 'seq').astype(jnp.bfloat16)  588 us
    ppermute x4, waiting for transfers between devices, partner(): return lax.ppermute(value, axis, pairs)  344 us
    select_n x4, other arithmetic, local(): jnp.where(lower_half, jnp.concatenate([gathered, partner_part], axis=1),...  53.2 us
  transfers between devices with their start and end apart: 6, of which 3 were waited for; matrix products, arithmetic and copies ran while one was open for 1% of the time, Pallas kernels for 0%

commit v1 on v0

v1 whole, which is shorter than its diff:
```python
import functools
import math

import jax
import jax.numpy as jnp
from jax import lax
from jax.experimental import pallas as pl
from jax.experimental.pallas import tpu as pltpu
from jax.sharding import PartitionSpec as P

HEADS = 8
HEAD_DIM = 128
BLOCK = 128
BLK_DEV = 3
SEG_DEV = 16
SEG_BLK = SEG_DEV * BLK_DEV
RING = 8
PLANE = 32
CHUNKS = 2 * BLK_DEV
EDGE = SEG_BLK
GLOBAL = SEG_BLK + 1
SLOTS = SEG_BLK + 3
SLICE = 16
MESH = pl.DeviceIdType.MESH


def remote(src, dst, send, recv, device):
    return pltpu.make_async_remote_copy(
        src_ref=src, dst_ref=dst, send_sem=send, recv_sem=recv, device_id=(device,), device_id_type=MESH
    )


def gather_kernel(
    owner_ref, kv_ref, cand_ref, out_ref, own, recv1, recv2, sel1, sel2,
    local_sem, ring_send, ring_recv, pair_send, pair_recv, edge_send, edge_recv,
    s1, r1, s2, r2, s3, r3,
):
    me = lax.axis_index("seq")
    core = me % 2
    z = me // 2 % RING
    seg = me // SEG_DEV
    plane = seg * 2 + core
    other = me + 1 - 2 * core
    home = me % SEG_DEV

    def at_z(zz):
        return seg * SEG_DEV + zz * 2 + core

    def at_plane(p):
        return p // 2 * SEG_DEV + z * 2 + p % 2

    barrier = pltpu.get_barrier_semaphore()

    @pl.loop(1, PLANE)
    def _(i):
        pl.semaphore_signal(barrier, inc=1, device_id=(at_plane((plane + i) % PLANE),), device_id_type=MESH)

    @pl.loop(1, RING)
    def _(i):
        pl.semaphore_signal(barrier, inc=1, device_id=(at_z((z + i) % RING),), device_id_type=MESH)

    pl.semaphore_wait(barrier, PLANE - 1 + RING - 1)

    def kv_chunk(q):
        return kv_ref.at[q // BLK_DEV, pl.ds(pl.multiple_of(q % BLK_DEV * BLOCK, BLOCK), BLOCK)]

    def slot(device, q):
        return out_ref.at[device * BLK_DEV + q % BLK_DEV, q // BLK_DEV]

    steps = (1, RING - 1)

    def ring(way, hop, q):
        held = (z + (hop - 1) * (RING - steps[way])) % RING * 2 + core
        src = kv_chunk(q) if hop == 1 else slot(held, q)
        return remote(
            src, slot(held, q), ring_send.at[way, hop - 1, q], ring_recv.at[way, hop - 1, q], at_z((z + steps[way]) % RING)
        )

    def came(way, hop, q):
        source = (z + hop * (RING - steps[way])) % RING * 2 + core
        here = slot(source, q)
        return remote(here, here, ring_send.at[way, hop - 1, q], ring_recv.at[way, hop - 1, q], other), source

    def pair(index, src, block, q):
        return remote(src, slot(block, q), pair_send.at[index, q], pair_recv.at[index, q], other)

    for q in range(CHUNKS):
        for way in range(2):
            ring(way, 1, q).start()
    bring = pltpu.make_async_copy(kv_ref, own, local_sem.at[0])
    bring.start()

    @pl.loop(1, PLANE)
    def _(i):
        to = (plane + i) % PLANE
        remote(cand_ref.at[to], recv1.at[plane], s1.at[to], r1.at[plane], at_plane(to)).start()

    mine = pltpu.make_async_copy(cand_ref.at[plane], recv1.at[plane], local_sem.at[1])
    mine.start()
    for q in range(CHUNKS):
        pair(0, kv_chunk(q), home, q).start()
    bring.wait()

    def keep(q):
        return pltpu.make_async_copy(
            own.at[q // BLK_DEV, pl.ds(q % BLK_DEV * BLOCK, BLOCK)], slot(home, q), local_sem.at[2 + q]
        )

    for q in range(CHUNKS):
        keep(q).start()

    def arrive(way, hop, q):
        got, source = came(way, hop, q)
        got.wait_recv()
        last = RING // 2 - 1
        if hop < last or (hop == last and (q < BLK_DEV) == (way == 0)):
            ring(way, hop + 1, q).start()
        index = hop if way == 0 or hop > last else hop + RING // 2
        pair(index, slot(source, q), source, q).start()

    def hop_of(hop):
        for q in range(CHUNKS):
            for way in range(2):
                if hop < RING // 2 or (q < BLK_DEV) == (way == 0):
                    arrive(way, hop, q)

    hop_of(1)

    def edge(block, kv, device):
        return remote(out_ref.at[block, kv], out_ref.at[EDGE, kv], edge_send.at[kv], edge_recv.at[kv], device)

    count = 16 * SEG_DEV
    up = (z == 0) & (core == 1)
    down = (z == RING - 1) & (core == 0)

    @pl.when(up)
    def _():
        for kv in range(2):
            edge(SEG_BLK - 1, kv, (me + SEG_DEV - 1) % count).start()

    @pl.when(down)
    def _():
        for kv in range(2):
            edge(0, kv, (me + count - SEG_DEV + 1) % count).start()

    mine.wait()

    @pl.loop(1, PLANE)
    def _(i):
        src = (plane + i) % PLANE
        remote(cand_ref.at[src], recv1.at[src], s1.at[src], r1.at[src], other).wait_recv()

    sel1[...] = recv1[owner_ref[0]]
    hop_of(2)

    @pl.loop(1, RING)
    def _(i):
        to = (z + i) % RING
        remote(sel1, recv2.at[z], s2.at[to], r2.at[z], at_z(to)).start()

    recv2[z] = sel1[...]

    @pl.loop(1, RING)
    def _(i):
        src = (z + i) % RING
        remote(sel1, recv2.at[src], s2.at[src], r2.at[src], other).wait_recv()

    sel2[...] = recv2[owner_ref[1]]

    def global_slot(p):
        return out_ref.at[
            GLOBAL + p // 16, p // 8 % 2, pl.ds(pl.multiple_of(p % 8 * SLICE, SLICE), SLICE)
        ]

    hop_of(3)

    @pl.loop(1, PLANE)
    def _(i):
        to = (plane + i) % PLANE
        remote(sel2, global_slot(plane), s3.at[to], r3.at[plane], at_plane(to)).start()

    own_slice = pltpu.make_async_copy(sel2, global_slot(plane), local_sem.at[1])
    own_slice.start()
    hop_of(4)

    own_slice.wait()
    for q in range(CHUNKS):
        keep(q).wait()

    @pl.loop(1, PLANE)
    def _(i):
        at = (plane + i) % PLANE
        remote(sel2, global_slot(at), s3.at[at], r3.at[at], other).wait_recv()
        remote(sel2, global_slot(plane), s3.at[at], r3.at[at], other).wait_send()
        remote(cand_ref.at[at], recv1.at[at], s1.at[at], r1.at[at], other).wait_send()

    @pl.loop(1, RING)
    def _(i):
        at = (z + i) % RING
        remote(sel1, recv2.at[at], s2.at[at], r2.at[at], other).wait_send()

    @pl.when((z == 0) & (core == 0) | (z == RING - 1) & (core == 1))
    def _():
        for kv in range(2):
            edge(0, kv, other).wait_recv()

    @pl.when(up | down)
    def _():
        for kv in range(2):
            edge(0, kv, other).wait_send()

    for q in range(CHUNKS):
        for way in range(2):
            for hop in range(1, RING // 2 + 1):
                if hop < RING // 2 or (q < BLK_DEV) == (way == 0):
                    ring(way, hop, q).wait_send()
        for index in range(RING):
            twin = home + 1 - 2 * core
            turn = index if index <= RING // 2 else RING - (index - RING // 2)
            block = (z + RING - turn) % RING * 2 + 1 - core if index else twin
            there = slot(block, q)
            copy = remote(there, there, pair_send.at[index, q], pair_recv.at[index, q], other)
            copy.wait_recv()
            copy.wait_send()


def gather(owner, kv, cand):
    dma = pltpu.SemaphoreType.DMA
    bf16 = jnp.bfloat16
    width = kv.shape[2]
    return pl.pallas_call(
        gather_kernel,
        out_shape=jax.ShapeDtypeStruct((SLOTS, 2, BLOCK, width), bf16),
        in_specs=[
            pl.BlockSpec(memory_space=pltpu.SMEM),
            pl.BlockSpec(memory_space=pl.ANY),
            pl.BlockSpec(memory_space=pl.ANY),
        ],
        out_specs=pl.BlockSpec(memory_space=pl.ANY),
        scratch_shapes=[
            pltpu.VMEM(kv.shape, bf16),
            pltpu.VMEM((PLANE, SLICE, width), bf16),
            pltpu.VMEM((RING, SLICE, width), bf16),
            pltpu.VMEM((SLICE, width), bf16),
            pltpu.VMEM((SLICE, width), bf16),
            dma((2 + CHUNKS,)),
            dma((2, RING // 2, CHUNKS)), dma((2, RING // 2, CHUNKS)),
            dma((RING, CHUNKS)), dma((RING, CHUNKS)),
            dma((2,)), dma((2,)),
            dma((PLANE,)), dma((PLANE,)),
            dma((RING,)), dma((RING,)),
            dma((PLANE,)), dma((PLANE,)),
        ],
        compiler_params=pltpu.CompilerParams(collective_id=0, has_side_effects=True),
        name="gather_blocks",
    )(owner, kv, cand)


def attend_kernel(table_ref, q_ref, *refs):
    kv_refs, (w_ref, o_ref, att) = refs[:8], refs[8:]
    scale = math.log2(math.e) / math.sqrt(HEAD_DIM)
    for head in range(HEADS):
        cols = pl.ds(head * HEAD_DIM, HEAD_DIM)
        keys = jnp.concatenate([ref[0, 0, :, cols] for ref in kv_refs], axis=0)
        values = jnp.concatenate([ref[0, 1, :, cols] for ref in kv_refs], axis=0)
        scores = lax.dot_general(
            q_ref[:, cols], keys, (((1,), (1,)), ((), ())), preferred_element_type=jnp.float32
        ) * scale
        top = jnp.max(scores, axis=1, keepdims=True)
        probs = jnp.exp2(scores - top)
        total = jnp.sum(probs, axis=1, keepdims=True)
        out = jnp.dot(probs.astype(jnp.bfloat16), values, preferred_element_type=jnp.float32)
        att[:, cols] = (out / total).astype(jnp.bfloat16)
    o_ref[...] = jnp.dot(att[...], w_ref[...], preferred_element_type=jnp.float32).astype(o_ref.dtype)


def attend(table, queries, blocks, weight):
    rows, width = queries.shape
    depth = weight.shape[1]

    def kv_spec(i):
        return pl.BlockSpec((1, 2, BLOCK, width), lambda b, t: (t[b * 8 + i], 0, 0, 0))

    return pl.pallas_call(
        attend_kernel,
        out_shape=jax.ShapeDtypeStruct((rows, depth), jnp.bfloat16),
        grid_spec=pltpu.PrefetchScalarGridSpec(
            num_scalar_prefetch=1,
            grid=(rows // BLOCK,),
            in_specs=[pl.BlockSpec((BLOCK, width), lambda b, t: (b, 0))]
            + [kv_spec(i) for i in range(8)]
            + [pl.BlockSpec((width, depth), lambda b, t: (0, 0), pipeline_mode=pl.Buffered(1))],
            out_specs=pl.BlockSpec((BLOCK, depth), lambda b, t: (b, 0)),
            scratch_shapes=[pltpu.VMEM((BLOCK, width), jnp.bfloat16)],
        ),
        compiler_params=pltpu.CompilerParams(vmem_limit_bytes=60 << 20),
        name="attend_blocks",
    )(table, queries, *([blocks] * 8), weight)


def local(queries, keys_values, rand_blocks, global_ids, out_weight):
    device = lax.axis_index("seq")
    home = device % SEG_DEV
    width = queries.shape[1]
    plane = device // SEG_DEV * 2 + device % 2
    owner = global_ids // BLK_DEV
    chosen = jnp.where(plane < PLANE // 2, owner[0], owner[1])
    owner_at = jnp.stack([chosen // SEG_DEV * 2 + chosen % 2, chosen // 2 % RING])
    cand = jnp.stack(
        [
            lax.dynamic_slice_in_dim(keys_values, global_ids[g] % BLK_DEV * BLOCK, BLOCK, 1)
            for g in range(2)
        ]
    ).reshape(PLANE, SLICE, width)
    blocks = gather(owner_at, keys_values, cand)
    first = home * BLK_DEV
    near = first + jnp.arange(BLK_DEV, dtype=jnp.int32)[:, None] + jnp.arange(-1, 2, dtype=jnp.int32)[None]
    near = jnp.where((near < 0) | (near >= SEG_BLK), EDGE, near)
    wide = jnp.broadcast_to(jnp.array([GLOBAL, GLOBAL + 1], jnp.int32), (BLK_DEV, 2))
    table = jnp.concatenate([near, wide, rand_blocks], axis=1).reshape(-1)
    return attend(table, queries, blocks, out_weight)


def solution(mesh):
    placed = (P("seq", None), P(None, "seq", None), P("seq", None), P(), P())
    return jax.shard_map(
        local, mesh=mesh, in_specs=placed, out_specs=P("seq", None), check_vma=False
    )
```

time: 1080 us -> 172 us (0.16)
  blocking collectives: 588 us -> 0 us
  waiting for transfers between devices: 344 us -> 0 us
  Pallas kernels: 0 us -> 162 us
  other arithmetic: 71.6 us -> 3.21 us
  local copies, waits for them, and re-layouts: 35.6 us -> 4.67 us
  matrix products: 28 us -> 0 us
  starting transfers between devices: 11.2 us -> 0 us
    psum x1 -> x0, blocking collectives: 588 us -> none  [local(): global_keys = lax.psum(masked_terms, 'seq').astype(jnp.bfloat16)]
    ppermute x6 -> x0, waiting for transfers between devices: 344 us -> none  [the longest x4 344 us: partner(): return lax.ppermute(value, axis, pairs)]
    pallas_call x0 -> x2, Pallas kernels: none -> 162 us  [the longest x1 145 us: gather(): pl.pallas_call(gather_kernel, out_shape=jax.ShapeDtypeStruct((SLOTS, 2, B...]
    select_n x6 -> x2, other arithmetic: 54.9 us -> 0.74 us  [the longest x1 0.67 us: local(): owner = global_ids // BLK_DEV]
    dot_general x3 -> x0, matrix products: 28 us -> none  [the longest x1 16.1 us: local(): jnp.einsum('nhqk,nkhd->nqhd', probs, all_keys[1], preferred_element_type=...]
    gather x2 -> x0, local copies, waits for them, and re-layouts: 14.7 us -> none  [local(): random_keys = jnp.take(segment_blocks, rand_blocks.reshape(-1), axis=1)]
    unnamed x15 -> x0, local copies, waits for them, and re-layouts: 13 us -> none
    ppermute x6 -> x0, starting transfers between devices: 11.2 us -> none  [the longest x4 9.87 us: partner(): return lax.ppermute(value, axis, pairs)]
  transfers between devices with their start and end apart: 6 -> 0, of which waited for: 3 -> 0; matrix products, arithmetic and copies ran while one was open for 1% -> 0% of each run, Pallas kernels for 0% -> 0%
where the time goes in v1:
time: 172 us
  Pallas kernels  162 us (94%)
  local copies, waits for them, and re-layouts  4.67 us (3%)
  other arithmetic  3.21 us (2%)
  between operations  2.63 us (2%)
    pallas_call x1, Pallas kernels, gather(): pl.pallas_call(gather_kernel, out_shape=jax.ShapeDtypeStruct((SLOTS, 2, B...  145 us
    pallas_call x1, Pallas kernels, attend(): pl.pallas_call(attend_kernel, out_shape=jax.ShapeDtypeStruct((rows, depth...  16.7 us

profile of v1, /device:TPU:1, one launch (start us, length us, event | category | flops | bytes accessed | tf_op | source)
XLA Modules:
  0.0 172.2 jit_solution(1538846044961147516)
XLA Ops:
  0.0 0.7 pad.5.clone
  0.7 0.7 and_select_fusion
  1.4 0.6 fusion.2
  3.3 0.7 pad_add_fusion.1.owner_ref
  4.0 0.1 add_select_fusion
  4.0 0.8 pad_add_fusion
  4.8 0.7 reshape.19.table_ref
  5.4 1.3 fusion.1
  8.1 1.4 dynamic-slice_bitcast_fusion.1
  9.4 1.1 pad_maximum_fusion
  10.5 145.0 %gather_blocks.1.refs_0_.refs_1_.refs_2_.refs_3_.refs_4_.refs_5_.refs_6_.refs_7_ = bf16[51,2,128,1024]{3,2,1,0:T(8,128)(2,1)} custom-call(s32[2]{0:T(128)} %pad_add_fusion.1.owner_ref, bf16[2,384,1024]{2,1,0:T(8,128)(2,1)} %kv_ref.1, bf16[32,16,1024]{2,1,0:T(8,128)(2,1)} %bitcast.11), custom_call_target="tpu_custom_call" | custom-call | tf_op jit(solution)/shard_map/gather_blocks/pallas_call | solution.py:231
  155.5 16.7 %attend_blocks.1 = bf16[384,2048]{1,0:T(8,128)(2,1)} custom-call(s32[24]{0:T(128)} %reshape.19.table_ref, bf16[384,1024]{1,0:T(8,128)(2,1)} %q_ref.1, bf16[51,2,128,1024]{3,2,1,0:T(8,128)(2,1)} %gather_blocks.1.refs_0_.refs_1_.refs_2_.refs_3_.refs_4_.refs_5_.refs_6_.refs_7_, ...), custom_call_target="tpu_custom_call" | custom-call | tf_op jit(solution)/shard_map/attend_blocks/pallas_call | solution.py:284
  (1 shorter events, 0.0 us)

commit v2 on v0

v2 whole, which is shorter than its diff:
```python
import math

import jax
import jax.numpy as jnp
from jax import lax
from jax.experimental import pallas as pl
from jax.experimental.pallas import tpu as pltpu
from jax.sharding import PartitionSpec as P

HEADS = 8
HEAD_DIM = 128
BLOCK = 128
BLK_DEV = 3
RAND = 3
GLOB = 2
SEG_DEV = 16
SEGS = 16
RING = 8
PLANE = 32
CHUNKS = 2 * BLK_DEV
ENTRIES = BLK_DEV * RAND
EDGE = 10 * BLK_DEV
SLICE = 16
ROOT = 13 * SEG_DEV
SCALE = math.log2(math.e) / math.sqrt(HEAD_DIM)
MESH = pl.DeviceIdType.MESH
OWN, L1, L2, S1, S2, L3 = range(6)


def remote(src, dst, send, recv, device):
    return pltpu.make_async_remote_copy(
        src_ref=src, dst_ref=dst, send_sem=send, recv_sem=recv, device_id=(device,), device_id_type=MESH
    )


def kernel(
    rand_ref, ids_ref, q_hbm, kv_hbm, w_hbm, out_hbm,
    near, l3k, l3v, far, last, stage3, stage4, own, cand, recv1, recv2, sel1, sel2, glob,
    q_ref, w_ref, o_ent, e_ent, o_win, e_win, att, out_ref,
    tab_ls, tab_lo, tab_ss, tab_so, slots, ranks,
    load_sem, long_s, long_r, short_s, short_r, sel_s, sel_r, pair_s, pair_r, tab_s, tab_r, edge_s, edge_r,
    s1, r1, s2, r2, s3, r3, s4, r4, all_in,
):
    me = lax.axis_index("seq")
    core = me % 2
    z = me // 2 % RING
    seg = me // SEG_DEV
    home = me % SEG_DEV
    plane = seg * 2 + core
    other = me + 1 - 2 * core
    go_long = 1 + (RING - 2) * core
    go_short = RING - go_long

    def hop(steps):
        return (z + steps) % RING

    def at(zz, cc):
        return seg * SEG_DEV + zz * 2 + cc

    def at_plane(p):
        return p // 2 * SEG_DEV + z * 2 + p % 2

    loads = [pltpu.make_async_copy(kv_hbm.at[:, j], near.at[j], load_sem.at[j]) for j in range(BLK_DEV)]
    loads += [pltpu.make_async_copy(kv_hbm.at[:, j], own.at[j], load_sem.at[BLK_DEV + j]) for j in range(BLK_DEV)]
    load_q = pltpu.make_async_copy(q_hbm, q_ref, load_sem.at[6])
    load_w = pltpu.make_async_copy(w_hbm, w_ref, load_sem.at[7])
    for copy in loads + [load_q, load_w]:
        copy.start()

    barrier = pltpu.get_barrier_semaphore()

    @pl.loop(1, SEG_DEV)
    def _(i):
        pl.semaphore_signal(
            barrier, inc=1, device_id=(seg * SEG_DEV + (home + i) % SEG_DEV,), device_id_type=MESH
        )

    @pl.when(me != ROOT)
    def _():
        pl.semaphore_wait(barrier, SEG_DEV - 1)

    @pl.when(me == ROOT)
    def _():
        pl.semaphore_wait(barrier, SEG_DEV - 1 + SEGS - 1)

    def mine(shard, q):
        kv, j = q // BLK_DEV, q % BLK_DEV
        if shard == L3:
            return (l3v if kv else l3k).at[j]
        return near.at[shard * BLK_DEV + j, kv]

    def theirs(shard, q):
        kv, j = q // BLK_DEV, q % BLK_DEV
        if shard == L3:
            return far.at[j, kv]
        return near.at[(5 + shard) * BLK_DEV + j, kv]

    longs, shorts = (OWN, L1, L2, L3), (OWN, S1, S2)

    def long(h, q):
        return remote(
            mine(longs[h - 1], q), mine(longs[h], q), long_s.at[h - 1, q], long_r.at[h - 1, q], at(hop(go_long), core)
        )

    def short(h, q):
        return remote(
            mine(shorts[h - 1], q), mine(shorts[h], q), short_s.at[h - 1, q], short_r.at[h - 1, q],
            at(hop(go_short), core),
        )

    def pair(shard, q):
        return remote(mine(shard, q), theirs(shard, q), pair_s.at[shard, q], pair_r.at[shard, q], other)

    for copy in loads[:BLK_DEV]:
        copy.wait()
    for q in range(CHUNKS):
        long(1, q).start()
        short(1, q).start()
    tables = [
        remote(rand_ref, tab_ss, tab_s.at[0], tab_r.at[0], at(hop(go_long), core)),
        remote(rand_ref, tab_ls, tab_s.at[1], tab_r.at[1], at(hop(go_short), core)),
        remote(rand_ref, tab_lo, tab_s.at[2], tab_r.at[2], at(hop(go_long), 1 - core)),
        remote(rand_ref, tab_so, tab_s.at[3], tab_r.at[3], at(hop(go_short), 1 - core)),
    ]
    for copy in tables:
        copy.start()
    for q in range(CHUNKS):
        pair(OWN, q).start()

    head = home == 0

    @pl.when(head & (me != ROOT))
    def _():
        pl.semaphore_signal(barrier, inc=1, device_id=(ROOT,), device_id_type=MESH)

    @pl.when(me == ROOT)
    def _():
        @pl.loop(1, SEGS)
        def _(i):
            pl.semaphore_signal(
                all_in, inc=1, device_id=((seg + i) % SEGS * SEG_DEV,), device_id_type=MESH
            )

    for copy in loads[BLK_DEV:]:
        copy.wait()
    for g in range(GLOB):
        block = ids_ref[g] % BLK_DEV
        for kv in range(2):
            cand[pl.ds((g * 2 + kv) * 8, 8)] = own[block, kv].reshape(8, SLICE, HEADS * HEAD_DIM)

    def code_of(value):
        device = value // BLK_DEV
        delta = (device // 2 + RING - z) % RING
        behind = (delta * core + (RING - delta) * (1 - core)) % RING
        same = jnp.where(device % 2 == core, 1, 0)
        return same, jnp.where(same == 1, behind, (RING - behind) % RING)

    values = [rand_ref[e // RAND, e % RAND] for e in range(ENTRIES)]
    keys = []
    for value in values:
        same, u = code_of(value)
        keys.append(jnp.minimum(u, RING - u) * 32 + u * 2 + same)
    for e in range(ENTRIES):
        ranks[e] = sum(jnp.where(keys[f] < keys[e], 1, 0) for f in range(ENTRIES) if f != e)
    held = [ranks[e] for e in range(ENTRIES)]
    for i in range(ENTRIES):
        slots[i] = sum(jnp.where(held[e] == i, values[e] * 4 + e // RAND, 0) for e in range(ENTRIES))

    @pl.when(head)
    def _():
        @pl.when(me != ROOT)
        def _():
            pl.semaphore_wait(all_in, 1)

        @pl.loop(1, SEG_DEV)
        def _(i):
            pl.semaphore_signal(all_in, inc=1, device_id=(seg * SEG_DEV + i,), device_id_type=MESH)

    @pl.when(home != 0)
    def _():
        pl.semaphore_wait(all_in, 1)

    @pl.loop(1, PLANE)
    def _(i):
        to = (plane + i) % PLANE
        remote(cand.at[to], recv1.at[plane], s1.at[to], r1.at[plane], at_plane(to)).start()

    recv1[plane] = cand[plane]

    which = plane // 16
    owner = ids_ref[0] * (1 - which) + ids_ref[1] * which
    owner = owner // BLK_DEV

    def cols_of(zz):
        return pl.ds(pl.multiple_of(zz * 128, 128), 128)

    def choose_in_plane():
        @pl.loop(1, PLANE)
        def _(i):
            src = (plane + i) % PLANE
            remote(cand.at[src], recv1.at[src], s1.at[src], r1.at[src], other).wait_recv()

        sel1[...] = recv1[owner // SEG_DEV * 2 + owner % 2]

    def scatter_z():
        @pl.loop(1, RING)
        def _(i):
            to = (z + i) % RING
            remote(sel1.at[:, cols_of(to)], recv2.at[z], s2.at[to], r2.at[z], at(to, core)).start()

        recv2[z] = sel1[:, cols_of(z)]

    def choose_in_ring():
        @pl.loop(1, RING)
        def _(i):
            src = (z + i) % RING
            remote(recv2.at[src], recv2.at[src], s2.at[src], r2.at[src], other).wait_recv()

        sel2[:, cols_of(z)] = recv2[owner // 2 % RING]

    def gather_z():
        piece = sel2.at[:, cols_of(z)]

        @pl.loop(1, RING)
        def _(i):
            to = (z + i) % RING
            remote(piece, piece, s3.at[to], r3.at[z], at(to, core)).start()

    def global_slot(p):
        return glob.at[p // 16, p // 8 % 2, pl.ds(pl.multiple_of(p % 8 * SLICE, SLICE), SLICE)]

    def spread_in_plane():
        @pl.loop(1, RING)
        def _(i):
            src = (z + i) % RING
            piece = sel2.at[:, cols_of(src)]
            remote(piece, piece, s3.at[src], r3.at[src], other).wait_recv()

        @pl.loop(1, PLANE)
        def _(i):
            to = (plane + i) % PLANE
            remote(sel2, global_slot(plane), s4.at[to], r4.at[plane], at_plane(to)).start()

        glob[plane // 16, plane // 8 % 2, pl.ds(pl.multiple_of(plane % 8 * SLICE, SLICE), SLICE)] = sel2[...]

    def global_here():
        @pl.loop(1, PLANE)
        def _(i):
            src = (plane + i) % PLANE
            remote(sel2, global_slot(src), s4.at[src], r4.at[src], other).wait_recv()

    def arrive_long(h, q):
        long(h, q).wait_recv()
        if h < 3:
            long(h + 1, q).start()
        pair(longs[h], q).start()

    def arrive_short(h, q):
        short(h, q).wait_recv()
        if h < 2:
            short(h + 1, q).start()
        pair(shorts[h], q).start()

    def wanted(table, source):
        got = 0
        for e in range(ENTRIES):
            value = table[e // RAND, e % RAND]
            got += jnp.where(value // BLK_DEV == source, value % BLK_DEV, 0)
        return got

    def send_sel(third, twin, kv):
        way = go_short if third == 0 else go_long
        stage = (stage3, stage4)[third]
        land = far.at[BLK_DEV + twin, kv] if third == 0 else last.at[twin, kv]
        to = at(hop(way), core if twin == 0 else 1 - core)
        return remote(stage.at[twin, kv], land, sel_s.at[third, twin, kv], sel_r.at[third, twin, kv], to)

    def columns(head_index):
        return pl.ds(head_index * HEAD_DIM, HEAD_DIM)

    def attend(query, key, value):
        scores = lax.dot_general(query, key, (((1,), (1,)), ((), ())), preferred_element_type=jnp.float32) * SCALE
        top = jnp.max(scores, axis=1, keepdims=True)
        probs = jnp.exp2(scores - top)
        total = jnp.sum(probs, axis=1, keepdims=True)
        out = jnp.dot(probs.astype(jnp.bfloat16), value, preferred_element_type=jnp.float32)
        return out / total, jnp.broadcast_to(top + jnp.log2(total), out.shape)

    def entry(i, group):
        packed = slots[i]
        row, value = packed % 4, packed // 4
        same, u = code_of(value)
        j = value % BLK_DEV
        place = jnp.where(u <= 2, u, jnp.where(u == 7, S1, S2))
        is_near = (u <= 2) | (u >= 6)
        near_at = jnp.where(is_near, ((1 - same) * 5 + place) * BLK_DEV + j, 0)
        is_l3 = (u == 3) & (same == 1)
        is_far = ((u == 3) & (same == 0)) | (u == 5)
        far_at = jnp.where(u == 5, BLK_DEV + 1 - same, j)
        for head_index in range(HEADS):
            cols = columns(head_index)

            def fetch(kv):
                got = near[near_at, kv, :, cols]
                if group >= 1:
                    got = jnp.where(is_l3, (l3v if kv else l3k)[j, :, cols], got)
                    got = jnp.where(is_far, far[far_at, kv, :, cols], got)
                if group >= 2:
                    got = jnp.where(u == 4, last[1 - same, kv, :, cols], got)
                return got

            out, weight = attend(q_ref[row, :, cols], fetch(0), fetch(1))
            o_ent[i, :, cols] = out
            e_ent[i, :, cols] = weight

    def window(b):
        edge_low = (z == 0) & (core == 0)
        edge_high = (z == RING - 1) & (core == 1)
        before = jnp.where(core == 0, (5 + S1) * BLK_DEV + 2, 5 * BLK_DEV + 2)
        before = jnp.where(edge_low, EDGE, before)
        after = jnp.where(core == 0, 5 * BLK_DEV, (5 + S1) * BLK_DEV)
        after = jnp.where(edge_high, EDGE, after)
        places = [before, 0, 1, 2, after][b : b + 3]
        for head_index in range(HEADS):
            cols = columns(head_index)

            def fetch(kv):
                return jnp.concatenate(
                    [near[p, kv, :, cols] for p in places] + [glob[g, kv, :, cols] for g in range(GLOB)], axis=0
                )

            out, weight = attend(q_ref[b, :, cols], fetch(0), fetch(1))
            o_win[b, :, cols] = out
            e_win[b, :, cols] = weight

    for q in range(CHUNKS):
        arrive_long(1, q)
        arrive_short(1, q)
        if q == 3:
            choose_in_plane()
        if q == 4:
            scatter_z()

    count = SEGS * SEG_DEV
    up = (z == 0) & (core == 1)
    down = (z == RING - 1) & (core == 0)

    def edge(kv, device):
        return remote(
            near.at[S1 * BLK_DEV + 2 * core, kv], near.at[EDGE, kv], edge_s.at[kv], edge_r.at[kv], device
        )

    @pl.when(up)
    def _():
        for kv in range(2):
            edge(kv, (me + SEG_DEV - 1) % count).start()

    @pl.when(down)
    def _():
        for kv in range(2):
            edge(kv, (me + count - SEG_DEV + 1) % count).start()

    for q in range(CHUNKS):
        arrive_long(2, q)
        arrive_short(2, q)
        if q == 2:
            choose_in_ring()
        if q == 3:
            gather_z()
    for q in range(CHUNKS):
        for shard in (OWN, L1, S1, L2, S2):
            pair(shard, q).wait_recv()

    @pl.when((z == 0) & (core == 0) | (z == RING - 1) & (core == 1))
    def _():
        for kv in range(2):
            edge(kv, other).wait_recv()

    for copy, table in zip(tables, (tab_ss, tab_ls, tab_lo, tab_so)):
        copy.wait_recv()
    source = hop(2 * go_long) * 2 + core
    for twin, table in enumerate((tab_ss, tab_so)):
        block = S2 * BLK_DEV + wanted(table, source)
        for kv in range(2):
            stage3[twin, kv] = near[block, kv]
    spread_in_plane()
    load_q.wait()
    for kv in range(2):
        for twin in range(2):
            send_sel(0, twin, kv).start()

    @pl.loop(0, 3)
    def _(i):
        entry(i, 0)

    source = hop(3 * go_short) * 2 + core
    picks = [wanted(table, source) for table in (tab_ls, tab_lo)]
    for q in range(BLK_DEV):
        arrive_long(3, q)
    for twin in range(2):
        stage4[twin, 0] = l3k[picks[twin]]
    global_here()
    window(0)
    for twin in range(2):
        send_sel(1, twin, 0).start()
    window(1)
    window(2)
    for q in range(BLK_DEV, CHUNKS):
        arrive_long(3, q)
    for twin in range(2):
        stage4[twin, 1] = l3v[picks[twin]]
    for q in range(CHUNKS):
        pair(L3, q).wait_recv()
    for twin in range(2):
        send_sel(1, twin, 1).start()
    for kv in range(2):
        for twin in range(2):
            send_sel(0, twin, kv).wait_recv()

    @pl.loop(3, 7)
    def _(i):
        entry(i, 1)

    for q in range(CHUNKS):
        for h in range(1, 4):
            long(h, q).wait_send()
        for h in range(1, 3):
            short(h, q).wait_send()
        for shard in range(6):
            pair(shard, q).wait_send()
    for copy in tables:
        copy.wait_send()

    @pl.when(up | down)
    def _():
        for kv in range(2):
            edge(kv, other).wait_send()

    @pl.loop(1, PLANE)
    def _(i):
        to = (plane + i) % PLANE
        remote(cand.at[to], recv1.at[to], s1.at[to], r1.at[to], other).wait_send()
        remote(sel2, global_slot(plane), s4.at[to], r4.at[to], other).wait_send()

    @pl.loop(1, RING)
    def _(i):
        to = (z + i) % RING
        piece = sel1.at[:, cols_of(to)]
        remote(piece, piece, s2.at[to], r2.at[to], other).wait_send()
        piece = sel2.at[:, cols_of(z)]
        remote(piece, piece, s3.at[to], r3.at[to], other).wait_send()

    load_w.wait()

    for kv in range(2):
        for twin in range(2):
            send_sel(1, twin, kv).wait_recv()

    @pl.loop(7, ENTRIES)
    def _(i):
        entry(i, 2)

    stores = []
    for b in range(BLK_DEV):
        rows = [ranks[b * RAND + r] for r in range(RAND)]
        for head_index in range(HEADS):
            cols = columns(head_index)
            outs = [o_win[b, :, cols]] + [o_ent[r, :, cols] for r in rows]
            logs = [e_win[b, :, cols]] + [e_ent[r, :, cols] for r in rows]
            top = jnp.maximum(jnp.maximum(logs[0], logs[1]), jnp.maximum(logs[2], logs[3]))
            weights = [jnp.exp2(log - top) for log in logs]
            out = sum(w * o for w, o in zip(weights, outs)) / sum(weights)
            att[b, :, cols] = out.astype(jnp.bfloat16)
        out_ref[b] = jnp.dot(att[b], w_ref[...], preferred_element_type=jnp.float32).astype(jnp.bfloat16)
        store = pltpu.make_async_copy(out_ref.at[b], out_hbm.at[b], load_sem.at[b])
        store.start()
        stores.append(store)
    for kv in range(2):
        for twin in range(2):
            send_sel(0, twin, kv).wait_send()
            send_sel(1, twin, kv).wait_send()
    for store in stores:
        store.wait()


def local(queries, keys_values, rand_blocks, global_ids, out_weight):
    width = queries.shape[1]
    depth = out_weight.shape[1]
    bf16, f32 = jnp.bfloat16, jnp.float32
    vmem, dma = pltpu.VMEM, pltpu.SemaphoreType.DMA
    table = pltpu.SMEM((BLK_DEV, RAND), jnp.int32)
    anywhere = pl.BlockSpec(memory_space=pl.ANY)
    scalars = pl.BlockSpec(memory_space=pltpu.SMEM)
    out = pl.pallas_call(
        kernel,
        out_shape=jax.ShapeDtypeStruct((BLK_DEV, BLOCK, depth), bf16),
        in_specs=[scalars, scalars, anywhere, anywhere, anywhere],
        out_specs=anywhere,
        scratch_shapes=[
            vmem((EDGE + 1, 2, BLOCK, width), bf16),
            vmem((BLK_DEV, BLOCK, width), bf16),
            vmem((BLK_DEV, BLOCK, width), bf16),
            vmem((BLK_DEV + 2, 2, BLOCK, width), bf16),
            vmem((2, 2, BLOCK, width), bf16),
            vmem((2, 2, BLOCK, width), bf16),
            vmem((2, 2, BLOCK, width), bf16),
            vmem((BLK_DEV, 2, BLOCK, width), bf16),
            vmem((PLANE, SLICE, width), bf16),
            vmem((PLANE, SLICE, width), bf16),
            vmem((RING, SLICE, 128), bf16),
            vmem((SLICE, width), bf16),
            vmem((SLICE, width), bf16),
            vmem((GLOB, 2, BLOCK, width), bf16),
            vmem((BLK_DEV, BLOCK, width), bf16),
            vmem((width, depth), bf16),
            vmem((ENTRIES, BLOCK, width), f32),
            vmem((ENTRIES, BLOCK, width), f32),
            vmem((BLK_DEV, BLOCK, width), f32),
            vmem((BLK_DEV, BLOCK, width), f32),
            vmem((BLK_DEV, BLOCK, width), bf16),
            vmem((BLK_DEV, BLOCK, depth), bf16),
            table, table, table, table,
            pltpu.SMEM((ENTRIES,), jnp.int32),
            pltpu.SMEM((ENTRIES,), jnp.int32),
            dma((8,)),
            dma((3, CHUNKS)), dma((3, CHUNKS)),
            dma((2, CHUNKS)), dma((2, CHUNKS)),
            dma((2, 2, 2)), dma((2, 2, 2)),
            dma((6, CHUNKS)), dma((6, CHUNKS)),
            dma((4,)), dma((4,)),
            dma((2,)), dma((2,)),
            dma((PLANE,)), dma((PLANE,)),
            dma((RING,)), dma((RING,)),
            dma((RING,)), dma((RING,)),
            dma((PLANE,)), dma((PLANE,)),
            pltpu.SemaphoreType.REGULAR,
        ],
        compiler_params=pltpu.CompilerParams(
            collective_id=0, has_side_effects=True, vmem_limit_bytes=60 << 20
        ),
        name="sparse_attention",
    )(
        rand_blocks,
        global_ids,
        queries.reshape(BLK_DEV, BLOCK, width),
        keys_values.reshape(2, BLK_DEV, BLOCK, width),
        out_weight,
    )
    return out.reshape(BLK_DEV * BLOCK, depth)


def solution(mesh):
    placed = (P("seq", None), P(None, "seq", None), P("seq", None), P(), P())
    return jax.shard_map(
        local, mesh=mesh, in_specs=placed, out_specs=P("seq", None), check_vma=False
    )
```

time: 1080 us -> 141 us (0.13)
  blocking collectives: 588 us -> 0 us
  waiting for transfers between devices: 344 us -> 0 us
  Pallas kernels: 0 us -> 138 us
  other arithmetic: 71.6 us -> 0 us
  local copies, waits for them, and re-layouts: 35.6 us -> 2.73 us
  matrix products: 28 us -> 0 us
  starting transfers between devices: 11.2 us -> 0 us
    psum x1 -> x0, blocking collectives: 588 us -> none  [local(): global_keys = lax.psum(masked_terms, 'seq').astype(jnp.bfloat16)]
    ppermute x6 -> x0, waiting for transfers between devices: 344 us -> none  [the longest x4 344 us: partner(): return lax.ppermute(value, axis, pairs)]
    pallas_call x0 -> x1, Pallas kernels: none -> 138 us  [local(): pl.pallas_call(kernel, out_shape=jax.ShapeDtypeStruct((BLK_DEV, BLOCK, de...]
    select_n x6 -> x0, other arithmetic: 54.9 us -> none  [the longest x4 53.2 us: local(): jnp.where(lower_half, jnp.concatenate([gathered, partner_part], axis=1),...]
    dot_general x3 -> x0, matrix products: 28 us -> none  [the longest x1 16.1 us: local(): jnp.einsum('nhqk,nkhd->nqhd', probs, all_keys[1], preferred_element_type=...]
    gather x2 -> x0, local copies, waits for them, and re-layouts: 14.7 us -> none  [local(): random_keys = jnp.take(segment_blocks, rand_blocks.reshape(-1), axis=1)]
    ppermute x6 -> x0, starting transfers between devices: 11.2 us -> none  [the longest x4 9.87 us: partner(): return lax.ppermute(value, axis, pairs)]
    sub x1 -> x0, other arithmetic: 11.1 us -> none  [local(): probs = jax.nn.softmax(scores, axis=-1).astype(jnp.bfloat16)]
  transfers between devices with their start and end apart: 6 -> 0, of which waited for: 3 -> 0; matrix products, arithmetic and copies ran while one was open for 1% -> 0% of each run, Pallas kernels for 0% -> 0%
where the time goes in v2:
time: 141 us
  Pallas kernels  138 us (98%)
  local copies, waits for them, and re-layouts  2.73 us (2%)
    pallas_call x1, Pallas kernels, local(): pl.pallas_call(kernel, out_shape=jax.ShapeDtypeStruct((BLK_DEV, BLOCK, de...  138 us

profile of v2, /device:TPU:1, one launch (start us, length us, event | category | flops | bytes accessed | tf_op | source)
XLA Modules:
  0.0 140.8 jit_solution(18042168397255782577)
XLA Ops:
  0.0 138.0 %sparse_attention.1 = bf16[3,128,2048]{2,1,0:T(8,128)(2,1)} custom-call(s32[3,3]{1,0:T(4,128)} %rand_ref.1, s32[2]{0:T(128)} %ids_ref.1, bf16[3,128,1024]{2,1,0:T(8,128)(2,1)} %bitcast.5, bf16[2,3,128,1024]{3,2,1,0:T(8,128)(2,1)} %bitcast.4, bf16[1024,2048]{1,0:T(8,128)(2,1)} %w_hbm.1), custom_call_target="tpu_custom_call" | custom-call | tf_op jit(solution)/shard_map/sparse_attention/pallas_call | solution.py:494
  138.1 2.7 %copy.7 = bf16[384,2048]{1,0:T(8,128)(2,1)} copy(bf16[384,2048]{1,0:T(8,128)(2,1)} %bitcast.3) | data formatting | bytes 3145728

commit v3 on v2

--- a/solution.py
+++ b/solution.py
@@ -35,7 +35,7 @@
 
 def kernel(
     rand_ref, ids_ref, q_hbm, kv_hbm, w_hbm, out_hbm,
-    near, l3k, l3v, far, last, stage3, stage4, own, cand, recv1, recv2, sel1, sel2, glob,
+    near, l3k, l3v, far, lastk, lastv, stage3, stage4, own, cand, recv1, recv2, sel1, sel2, glob,
     q_ref, w_ref, o_ent, e_ent, o_win, e_win, att, out_ref,
     tab_ls, tab_lo, tab_ss, tab_so, slots, ranks,
     load_sem, long_s, long_r, short_s, short_r, sel_s, sel_r, pair_s, pair_r, tab_s, tab_r, edge_s, edge_r,
@@ -271,22 +271,33 @@
     def send_sel(third, twin, kv):
         way = go_short if third == 0 else go_long
         stage = (stage3, stage4)[third]
-        land = far.at[BLK_DEV + twin, kv] if third == 0 else last.at[twin, kv]
+        land = far.at[BLK_DEV + twin, kv] if third == 0 else (lastv if kv else lastk).at[twin]
         to = at(hop(way), core if twin == 0 else 1 - core)
         return remote(stage.at[twin, kv], land, sel_s.at[third, twin, kv], sel_r.at[third, twin, kv], to)
 
     def columns(head_index):
         return pl.ds(head_index * HEAD_DIM, HEAD_DIM)
 
-    def attend(query, key, value):
-        scores = lax.dot_general(query, key, (((1,), (1,)), ((), ())), preferred_element_type=jnp.float32) * SCALE
-        top = jnp.max(scores, axis=1, keepdims=True)
-        probs = jnp.exp2(scores - top)
-        total = jnp.sum(probs, axis=1, keepdims=True)
-        out = jnp.dot(probs.astype(jnp.bfloat16), value, preferred_element_type=jnp.float32)
-        return out / total, jnp.broadcast_to(top + jnp.log2(total), out.shape)
-
-    def entry(i, group):
+    def weigh(queries, keys):
+        scores = [
+            lax.dot_general(query, key, (((1,), (1,)), ((), ())), preferred_element_type=jnp.float32)
+            for query, key in zip(queries, keys)
+        ]
+        tops = [jnp.max(score, axis=1, keepdims=True) for score in scores]
+        probs = [jnp.exp2((score - top) * SCALE) for score, top in zip(scores, tops)]
+        totals = [jnp.sum(prob, axis=1, keepdims=True) for prob in probs]
+        return [prob.astype(jnp.bfloat16) for prob in probs], tops, totals
+
+    def collect(weighed, values, head_indices, o_ref, e_ref):
+        probs, tops, totals = weighed
+        outs = [jnp.dot(prob, value, preferred_element_type=jnp.float32) for prob, value in zip(probs, values)]
+        for head_index, out, top, total in zip(head_indices, outs, tops, totals):
+            o_ref[:, columns(head_index)] = out / total
+            e_ref[:, columns(head_index)] = jnp.broadcast_to(top * SCALE + jnp.log2(total), out.shape)
+
+    heads = range(HEADS)
+
+    def entry_parts(i, group):
         packed = slots[i]
         row, value = packed % 4, packed // 4
         same, u = code_of(value)
@@ -297,21 +308,28 @@
         is_l3 = (u == 3) & (same == 1)
         is_far = ((u == 3) & (same == 0)) | (u == 5)
         far_at = jnp.where(u == 5, BLK_DEV + 1 - same, j)
-        for head_index in range(HEADS):
+
+        def fetch(head_index, kv):
             cols = columns(head_index)
-
-            def fetch(kv):
-                got = near[near_at, kv, :, cols]
-                if group >= 1:
-                    got = jnp.where(is_l3, (l3v if kv else l3k)[j, :, cols], got)
-                    got = jnp.where(is_far, far[far_at, kv, :, cols], got)
-                if group >= 2:
-                    got = jnp.where(u == 4, last[1 - same, kv, :, cols], got)
-                return got
-
-            out, weight = attend(q_ref[row, :, cols], fetch(0), fetch(1))
-            o_ent[i, :, cols] = out
-            e_ent[i, :, cols] = weight
+            got = near[near_at, kv, :, cols]
+            if group >= 1:
+                got = jnp.where(is_l3, (l3v if kv else l3k)[j, :, cols], got)
+                got = jnp.where(is_far, far[far_at, kv, :, cols], got)
+            if group >= 2:
+                got = jnp.where(u == 4, (lastv if kv else lastk)[1 - same, :, cols], got)
+            return got
+
+        def first():
+            return weigh([q_ref[row, :, columns(h)] for h in heads], [fetch(h, 0) for h in heads])
+
+        def second(weighed):
+            collect(weighed, [fetch(h, 1) for h in heads], heads, o_ent.at[i], e_ent.at[i])
+
+        return first, second
+
+    def entry(i, group):
+        first, second = entry_parts(i, group)
+        second(first())
 
     def window(b):
         edge_low = (z == 0) & (core == 0)
@@ -321,24 +339,23 @@
         after = jnp.where(core == 0, 5 * BLK_DEV, (5 + S1) * BLK_DEV)
         after = jnp.where(edge_high, EDGE, after)
         places = [before, 0, 1, 2, after][b : b + 3]
-        for head_index in range(HEADS):
+
+        def fetch(head_index, kv):
             cols = columns(head_index)
-
-            def fetch(kv):
-                return jnp.concatenate(
-                    [near[p, kv, :, cols] for p in places] + [glob[g, kv, :, cols] for g in range(GLOB)], axis=0
-                )
-
-            out, weight = attend(q_ref[b, :, cols], fetch(0), fetch(1))
-            o_win[b, :, cols] = out
-            e_win[b, :, cols] = weight
+            return jnp.concatenate(
+                [near[p, kv, :, cols] for p in places] + [glob[g, kv, :, cols] for g in range(GLOB)], axis=0
+            )
+
+        for some in (heads[: HEADS // 2], heads[HEADS // 2 :]):
+            weighed = weigh([q_ref[b, :, columns(h)] for h in some], [fetch(h, 0) for h in some])
+            collect(weighed, [fetch(h, 1) for h in some], some, o_win.at[b], e_win.at[b])
 
     for q in range(CHUNKS):
         arrive_long(1, q)
         arrive_short(1, q)
-        if q == 3:
+        if q == 1:
             choose_in_plane()
-        if q == 4:
+        if q == 2:
             scatter_z()
 
     count = SEGS * SEG_DEV
@@ -363,9 +380,9 @@
     for q in range(CHUNKS):
         arrive_long(2, q)
         arrive_short(2, q)
-        if q == 2:
+        if q == 0:
             choose_in_ring()
-        if q == 3:
+        if q == 1:
             gather_z()
     for q in range(CHUNKS):
         for shard in (OWN, L1, S1, L2, S2):
@@ -383,15 +400,19 @@
         block = S2 * BLK_DEV + wanted(table, source)
         for kv in range(2):
             stage3[twin, kv] = near[block, kv]
-    spread_in_plane()
     load_q.wait()
     for kv in range(2):
         for twin in range(2):
             send_sel(0, twin, kv).start()
+    spread_in_plane()
 
     @pl.loop(0, 3)
     def _(i):
         entry(i, 0)
+
+    global_here()
+    for b in range(BLK_DEV):
+        window(b)
 
     source = hop(3 * go_short) * 2 + core
     picks = [wanted(table, source) for table in (tab_ls, tab_lo)]
@@ -399,23 +420,21 @@
         arrive_long(3, q)
     for twin in range(2):
         stage4[twin, 0] = l3k[picks[twin]]
-    global_here()
-    window(0)
+    for q in range(BLK_DEV):
+        pair(L3, q).wait_recv()
     for twin in range(2):
         send_sel(1, twin, 0).start()
-    window(1)
-    window(2)
     for q in range(BLK_DEV, CHUNKS):
         arrive_long(3, q)
     for twin in range(2):
         stage4[twin, 1] = l3v[picks[twin]]
-    for q in range(CHUNKS):
-        pair(L3, q).wait_recv()
-    for twin in range(2):
-        send_sel(1, twin, 1).start()
     for kv in range(2):
         for twin in range(2):
             send_sel(0, twin, kv).wait_recv()
+    for twin in range(2):
+        send_sel(1, twin, 1).start()
+    for q in range(BLK_DEV, CHUNKS):
+        pair(L3, q).wait_recv()
 
     @pl.loop(3, 7)
     def _(i):
@@ -452,13 +471,14 @@
 
     load_w.wait()
 
-    for kv in range(2):
-        for twin in range(2):
-            send_sel(1, twin, kv).wait_recv()
-
-    @pl.loop(7, ENTRIES)
-    def _(i):
-        entry(i, 2)
+    for twin in range(2):
+        send_sel(1, twin, 0).wait_recv()
+    ends = [entry_parts(i, 2) for i in range(7, ENTRIES)]
+    halves = [first() for first, _ in ends]
+    for twin in range(2):
+        send_sel(1, twin, 1).wait_recv()
+    for (_, second), half in zip(ends, halves):
+        second(half)
 
     stores = []
     for b in range(BLK_DEV):
@@ -501,7 +521,8 @@
             vmem((BLK_DEV, BLOCK, width), bf16),
             vmem((BLK_DEV, BLOCK, width), bf16),
             vmem((BLK_DEV + 2, 2, BLOCK, width), bf16),
-            vmem((2, 2, BLOCK, width), bf16),
+            vmem((2, BLOCK, width), bf16),
+            vmem((2, BLOCK, width), bf16),
             vmem((2, 2, BLOCK, width), bf16),
             vmem((2, 2, BLOCK, width), bf16),
             vmem((BLK_DEV, 2, BLOCK, width), bf16),

time: 141 us -> 134 us (0.950); the launches traced: 141 us -> 132 us
  Pallas kernels: 138 us -> 129 us
    pallas_call x1, Pallas kernels: 138 us -> 129 us  [local(): pl.pallas_call(kernel, out_shape=jax.ShapeDtypeStruct((BLK_DEV, BLOCK, de...]
where the time goes in v3:
time: 134 us; the launch traced here: 132 us
  Pallas kernels  129 us (96%)
  local copies, waits for them, and re-layouts  2.73 us (2%)
    pallas_call x1, Pallas kernels, local(): pl.pallas_call(kernel, out_shape=jax.ShapeDtypeStruct((BLK_DEV, BLOCK, de...  129 us
    unnamed x1, local copies, waits for them, and re-layouts  2.73 us

profile of v3, /device:TPU:1, one launch (start us, length us, event | category | flops | bytes accessed | tf_op | source)
XLA Modules:
  0.0 132.1 jit_solution(987526140963483986)
XLA Ops:
  0.0 129.4 %sparse_attention.1 = bf16[3,128,2048]{2,1,0:T(8,128)(2,1)} custom-call(s32[3,3]{1,0:T(4,128)} %rand_ref.1, s32[2]{0:T(128)} %ids_ref.1, bf16[3,128,1024]{2,1,0:T(8,128)(2,1)} %bitcast.5, bf16[2,3,128,1024]{3,2,1,0:T(8,128)(2,1)} %bitcast.4, bf16[1024,2048]{1,0:T(8,128)(2,1)} %w_hbm.1), custom_call_target="tpu_custom_call" | custom-call | tf_op jit(solution)/shard_map/sparse_attention/pallas_call | solution.py:514
  129.4 2.7 %copy.7 = bf16[384,2048]{1,0:T(8,128)(2,1)} copy(bf16[384,2048]{1,0:T(8,128)(2,1)} %bitcast.3) | data formatting | bytes 3145728

commit v4 on v3

--- a/solution.py
+++ b/solution.py
@@ -34,12 +34,12 @@
 
 
 def kernel(
-    rand_ref, ids_ref, q_hbm, kv_hbm, w_hbm, out_hbm,
+    rand_ref, ids_ref, q_hbm, kv_hbm, w_hbm, out_ref,
     near, l3k, l3v, far, lastk, lastv, stage3, stage4, own, cand, recv1, recv2, sel1, sel2, glob,
-    q_ref, w_ref, o_ent, e_ent, o_win, e_win, att, out_ref,
+    q_ref, w_ref, o_ent, e_ent, o_win, e_win, att,
     tab_ls, tab_lo, tab_ss, tab_so, slots, ranks,
     load_sem, long_s, long_r, short_s, short_r, sel_s, sel_r, pair_s, pair_r, tab_s, tab_r, edge_s, edge_r,
-    s1, r1, s2, r2, s3, r3, s4, r4, all_in,
+    s1, r1, s2, r2, s3, r3, s4, r4, all_in, greet, chain,
 ):
     me = lax.axis_index("seq")
     core = me % 2
@@ -69,19 +69,26 @@
 
     barrier = pltpu.get_barrier_semaphore()
 
-    @pl.loop(1, SEG_DEV)
-    def _(i):
-        pl.semaphore_signal(
-            barrier, inc=1, device_id=(seg * SEG_DEV + (home + i) % SEG_DEV,), device_id_type=MESH
-        )
+    greeted = [other] + [at(hop(step), cc) for step in (go_long, go_short) for cc in (core, 1 - core)]
+    for device in greeted:
+
+        @pl.when((device != ROOT) | (me == ROOT))
+        def _(device=device):
+            pl.semaphore_signal(barrier, inc=1, device_id=(device,), device_id_type=MESH)
 
     @pl.when(me != ROOT)
     def _():
-        pl.semaphore_wait(barrier, SEG_DEV - 1)
+        pl.semaphore_wait(barrier, len(greeted))
+
+    for device in greeted:
+
+        @pl.when(device == ROOT)
+        def _(device=device):
+            pl.semaphore_signal(greet, inc=1, device_id=(device,), device_id_type=MESH)
 
     @pl.when(me == ROOT)
     def _():
-        pl.semaphore_wait(barrier, SEG_DEV - 1 + SEGS - 1)
+        pl.semaphore_wait(greet, len(greeted))
 
     def mine(shard, q):
         kv, j = q // BLK_DEV, q % BLK_DEV
@@ -128,6 +135,20 @@
         pair(OWN, q).start()
 
     head = home == 0
+    middle = RING // 2
+
+    @pl.when(head)
+    def _():
+        pl.semaphore_wait(chain, 2)
+
+    @pl.when((core == 0) & (z != 0) & (z != middle) & (z != middle + 1))
+    def _():
+        pl.semaphore_wait(chain, 1)
+
+    @pl.when((core == 0) & (z != 0))
+    def _():
+        towards = jnp.where(z <= middle, z - 1, hop(1))
+        pl.semaphore_signal(chain, inc=1, device_id=(at(towards, 0),), device_id_type=MESH)
 
     @pl.when(head & (me != ROOT))
     def _():
@@ -135,6 +156,8 @@
 
     @pl.when(me == ROOT)
     def _():
+        pl.semaphore_wait(barrier, SEGS - 1)
+
         @pl.loop(1, SEGS)
         def _(i):
             pl.semaphore_signal(
@@ -480,7 +503,6 @@
     for (_, second), half in zip(ends, halves):
         second(half)
 
-    stores = []
     for b in range(BLK_DEV):
         rows = [ranks[b * RAND + r] for r in range(RAND)]
         for head_index in range(HEADS):
@@ -492,15 +514,28 @@
             out = sum(w * o for w, o in zip(weights, outs)) / sum(weights)
             att[b, :, cols] = out.astype(jnp.bfloat16)
         out_ref[b] = jnp.dot(att[b], w_ref[...], preferred_element_type=jnp.float32).astype(jnp.bfloat16)
-        store = pltpu.make_async_copy(out_ref.at[b], out_hbm.at[b], load_sem.at[b])
-        store.start()
-        stores.append(store)
     for kv in range(2):
         for twin in range(2):
             send_sel(0, twin, kv).wait_send()
             send_sel(1, twin, kv).wait_send()
-    for store in stores:
-        store.wait()
+
+
+def put_kernel(x_ref, out_ref, sem):
+    copy = pltpu.make_async_copy(x_ref, out_ref, sem)
+    copy.start()
+    copy.wait()
+
+
+def put(x):
+    return pl.pallas_call(
+        put_kernel,
+        out_shape=jax.ShapeDtypeStruct(x.shape, x.dtype),
+        in_specs=[pl.BlockSpec(memory_space=pltpu.VMEM)],
+        out_specs=pl.BlockSpec(memory_space=pltpu.HBM),
+        scratch_shapes=[pltpu.SemaphoreType.DMA],
+        compiler_params=pltpu.CompilerParams(vmem_limit_bytes=4 << 20),
+        name="put",
+    )(x)
 
 
 def local(queries, keys_values, rand_blocks, global_ids, out_weight):
@@ -509,13 +544,13 @@
     bf16, f32 = jnp.bfloat16, jnp.float32
     vmem, dma = pltpu.VMEM, pltpu.SemaphoreType.DMA
     table = pltpu.SMEM((BLK_DEV, RAND), jnp.int32)
-    anywhere = pl.BlockSpec(memory_space=pl.ANY)
+    in_hbm = pl.BlockSpec(memory_space=pltpu.HBM)
     scalars = pl.BlockSpec(memory_space=pltpu.SMEM)
     out = pl.pallas_call(
         kernel,
-        out_shape=jax.ShapeDtypeStruct((BLK_DEV, BLOCK, depth), bf16),
-        in_specs=[scalars, scalars, anywhere, anywhere, anywhere],
-        out_specs=anywhere,
+        out_shape=pltpu.VMEM((BLK_DEV, BLOCK, depth), bf16),
+        in_specs=[scalars, scalars, in_hbm, in_hbm, in_hbm],
+        out_specs=pl.BlockSpec(memory_space=pltpu.VMEM),
         scratch_shapes=[
             vmem((EDGE + 1, 2, BLOCK, width), bf16),
             vmem((BLK_DEV, BLOCK, width), bf16),
@@ -539,7 +574,6 @@
             vmem((BLK_DEV, BLOCK, width), f32),
             vmem((BLK_DEV, BLOCK, width), f32),
             vmem((BLK_DEV, BLOCK, width), bf16),
-            vmem((BLK_DEV, BLOCK, depth), bf16),
             table, table, table, table,
             pltpu.SMEM((ENTRIES,), jnp.int32),
             pltpu.SMEM((ENTRIES,), jnp.int32),
@@ -555,9 +589,11 @@
             dma((RING,)), dma((RING,)),
             dma((PLANE,)), dma((PLANE,)),
             pltpu.SemaphoreType.REGULAR,
+            pltpu.SemaphoreType.REGULAR,
+            pltpu.SemaphoreType.REGULAR,
         ],
         compiler_params=pltpu.CompilerParams(
-            collective_id=0, has_side_effects=True, vmem_limit_bytes=60 << 20
+            collective_id=0, has_side_effects=True, vmem_limit_bytes=56 << 20
         ),
         name="sparse_attention",
     )(
@@ -567,7 +603,7 @@
         keys_values.reshape(2, BLK_DEV, BLOCK, width),
         out_weight,
     )
-    return out.reshape(BLK_DEV * BLOCK, depth)
+    return put(out.reshape(BLK_DEV * BLOCK, depth))
 
 
 def solution(mesh):

time: 134 us -> 132 us (0.985)
  local copies, waits for them, and re-layouts: 2.73 us -> 0 us
    unnamed x1 -> x0, local copies, waits for them, and re-layouts: 2.73 us -> none
    pallas_call x1 -> x2, Pallas kernels: 129 us -> 130 us  [the longest x1 129 us: local(): pl.pallas_call(kernel, out_shape=pltpu.VMEM((BLK_DEV, BLOCK, depth), bf16...]
where the time goes in v4:
time: 132 us; the launch traced here: 130 us
  Pallas kernels  130 us (98%)
    pallas_call x1, Pallas kernels, local(): pl.pallas_call(kernel, out_shape=pltpu.VMEM((BLK_DEV, BLOCK, depth), bf16...  129 us

profile of v4, /device:TPU:1, one launch (start us, length us, event | category | flops | bytes accessed | tf_op | source)
XLA Modules:
  0.0 129.7 jit_solution(3680628277970462581)
XLA Ops:
  0.0 128.5 %sparse_attention.1 = bf16[3,128,2048]{2,1,0:T(8,128)(2,1)S(1)} custom-call(s32[3,3]{1,0:T(4,128)} %rand_ref.1, s32[2]{0:T(128)} %ids_ref.1, bf16[3,128,1024]{2,1,0:T(8,128)(2,1)} %bitcast.5, bf16[2,3,128,1024]{3,2,1,0:T(8,128)(2,1)} %bitcast.4, bf16[1024,2048]{1,0:T(8,128)(2,1)} %w_hbm.1), custom_call_target="tpu_custom_call" | custom-call | tf_op jit(solution)/shard_map/sparse_attention/pallas_call | solution.py:549
  128.6 1.2 put.1

commit v5 on v4

--- a/solution.py
+++ b/solution.py
@@ -35,7 +35,7 @@
 
 def kernel(
     rand_ref, ids_ref, q_hbm, kv_hbm, w_hbm, out_ref,
-    near, l3k, l3v, far, lastk, lastv, stage3, stage4, own, cand, recv1, recv2, sel1, sel2, glob,
+    near, l3k, l3v, far, lastk, lastv, stage3, stage4, own, cand, recv1, recv2, sel1, piece, sel2, glob,
     q_ref, w_ref, o_ent, e_ent, o_win, e_win, att,
     tab_ls, tab_lo, tab_ss, tab_so, slots, ranks,
     load_sem, long_s, long_r, short_s, short_r, sel_s, sel_r, pair_s, pair_r, tab_s, tab_r, edge_s, edge_r,
@@ -239,37 +239,39 @@
             src = (z + i) % RING
             remote(recv2.at[src], recv2.at[src], s2.at[src], r2.at[src], other).wait_recv()
 
-        sel2[:, cols_of(z)] = recv2[owner // 2 % RING]
+        piece[...] = recv2[owner // 2 % RING]
+
+    def along_x(step):
+        return seg // 4 * 4 + (seg + step) % 4
+
+    slot = along_x(3) * 2 + core
 
     def gather_z():
-        piece = sel2.at[:, cols_of(z)]
-
-        @pl.loop(1, RING)
-        def _(i):
-            to = (z + i) % RING
-            remote(piece, piece, s3.at[to], r3.at[z], at(to, core)).start()
+        @pl.loop(0, RING)
+        def _(to):
+            there = along_x(1) * SEG_DEV + to * 2 + core
+            remote(piece, sel2.at[:, cols_of(z)], s3.at[to], r3.at[z], there).start()
 
     def global_slot(p):
         return glob.at[p // 16, p // 8 % 2, pl.ds(pl.multiple_of(p % 8 * SLICE, SLICE), SLICE)]
 
     def spread_in_plane():
-        @pl.loop(1, RING)
-        def _(i):
-            src = (z + i) % RING
-            piece = sel2.at[:, cols_of(src)]
-            remote(piece, piece, s3.at[src], r3.at[src], other).wait_recv()
+        @pl.loop(0, RING)
+        def _(src):
+            there = sel2.at[:, cols_of(src)]
+            remote(there, there, s3.at[src], r3.at[src], other).wait_recv()
 
         @pl.loop(1, PLANE)
         def _(i):
             to = (plane + i) % PLANE
-            remote(sel2, global_slot(plane), s4.at[to], r4.at[plane], at_plane(to)).start()
-
-        glob[plane // 16, plane // 8 % 2, pl.ds(pl.multiple_of(plane % 8 * SLICE, SLICE), SLICE)] = sel2[...]
+            remote(sel2, global_slot(slot), s4.at[to], r4.at[slot], at_plane(to)).start()
+
+        glob[slot // 16, slot // 8 % 2, pl.ds(pl.multiple_of(slot % 8 * SLICE, SLICE), SLICE)] = sel2[...]
 
     def global_here():
         @pl.loop(1, PLANE)
         def _(i):
-            src = (plane + i) % PLANE
+            src = (slot + i) % PLANE
             remote(sel2, global_slot(src), s4.at[src], r4.at[src], other).wait_recv()
 
     def arrive_long(h, q):
@@ -407,6 +409,8 @@
             choose_in_ring()
         if q == 1:
             gather_z()
+        if q == 4:
+            spread_in_plane()
     for q in range(CHUNKS):
         for shard in (OWN, L1, S1, L2, S2):
             pair(shard, q).wait_recv()
@@ -427,7 +431,6 @@
     for kv in range(2):
         for twin in range(2):
             send_sel(0, twin, kv).start()
-    spread_in_plane()
 
     @pl.loop(0, 3)
     def _(i):
@@ -443,32 +446,58 @@
         arrive_long(3, q)
     for twin in range(2):
         stage4[twin, 0] = l3k[picks[twin]]
-    for q in range(BLK_DEV):
-        pair(L3, q).wait_recv()
+
+    @pl.loop(1, PLANE)
+    def _(i):
+        to = (plane + i) % PLANE
+        remote(cand.at[to], recv1.at[to], s1.at[to], r1.at[to], other).wait_send()
+        remote(sel2, global_slot(slot), s4.at[to], r4.at[to], other).wait_send()
+
     for twin in range(2):
         send_sel(1, twin, 0).start()
     for q in range(BLK_DEV, CHUNKS):
         arrive_long(3, q)
     for twin in range(2):
         stage4[twin, 1] = l3v[picks[twin]]
+    for q in range(CHUNKS):
+        long(1, q).wait_send()
+        short(1, q).wait_send()
+        pair(OWN, q).wait_send()
+    for twin in range(2):
+        send_sel(1, twin, 1).start()
+    for q in range(CHUNKS):
+        pair(L3, q).wait_recv()
     for kv in range(2):
         for twin in range(2):
             send_sel(0, twin, kv).wait_recv()
-    for twin in range(2):
-        send_sel(1, twin, 1).start()
-    for q in range(BLK_DEV, CHUNKS):
-        pair(L3, q).wait_recv()
 
     @pl.loop(3, 7)
     def _(i):
         entry(i, 1)
 
-    for q in range(CHUNKS):
-        for h in range(1, 4):
+    def merge(outs, logs):
+        top = logs[0]
+        for log in logs[1:]:
+            top = jnp.maximum(top, log)
+        weights = [jnp.exp2(log - top) for log in logs]
+        total = sum(weights)
+        return sum(weight * out for weight, out in zip(weights, outs)), total, top
+
+    for b in range(BLK_DEV):
+        rows = [ranks[b * RAND + r] for r in range(RAND)]
+        for head_index in range(HEADS):
+            cols = columns(head_index)
+            outs = [o_win[b, :, cols]] + [jnp.where(r < 7, o_ent[r, :, cols], 0.0) for r in rows]
+            logs = [e_win[b, :, cols]] + [jnp.where(r < 7, e_ent[r, :, cols], -jnp.inf) for r in rows]
+            out, total, top = merge(outs, logs)
+            o_win[b, :, cols] = out / total
+            e_win[b, :, cols] = top + jnp.log2(total)
+
+    for q in range(CHUNKS):
+        for h in range(2, 4):
             long(h, q).wait_send()
-        for h in range(1, 3):
-            short(h, q).wait_send()
-        for shard in range(6):
+        short(2, q).wait_send()
+        for shard in range(1, 6):
             pair(shard, q).wait_send()
     for copy in tables:
         copy.wait_send()
@@ -478,18 +507,14 @@
         for kv in range(2):
             edge(kv, other).wait_send()
 
-    @pl.loop(1, PLANE)
-    def _(i):
-        to = (plane + i) % PLANE
-        remote(cand.at[to], recv1.at[to], s1.at[to], r1.at[to], other).wait_send()
-        remote(sel2, global_slot(plane), s4.at[to], r4.at[to], other).wait_send()
-
     @pl.loop(1, RING)
     def _(i):
         to = (z + i) % RING
-        piece = sel1.at[:, cols_of(to)]
-        remote(piece, piece, s2.at[to], r2.at[to], other).wait_send()
-        piece = sel2.at[:, cols_of(z)]
+        there = sel1.at[:, cols_of(to)]
+        remote(there, there, s2.at[to], r2.at[to], other).wait_send()
+
+    @pl.loop(0, RING)
+    def _(to):
         remote(piece, piece, s3.at[to], r3.at[to], other).wait_send()
 
     load_w.wait()
@@ -504,16 +529,19 @@
         second(half)
 
     for b in range(BLK_DEV):
-        rows = [ranks[b * RAND + r] for r in range(RAND)]
+        here = [slots[i] % 4 == b for i in range(7, ENTRIES)]
         for head_index in range(HEADS):
             cols = columns(head_index)
-            outs = [o_win[b, :, cols]] + [o_ent[r, :, cols] for r in rows]
-            logs = [e_win[b, :, cols]] + [e_ent[r, :, cols] for r in rows]
-            top = jnp.maximum(jnp.maximum(logs[0], logs[1]), jnp.maximum(logs[2], logs[3]))
-            weights = [jnp.exp2(log - top) for log in logs]
-            out = sum(w * o for w, o in zip(weights, outs)) / sum(weights)
-            att[b, :, cols] = out.astype(jnp.bfloat16)
-        out_ref[b] = jnp.dot(att[b], w_ref[...], preferred_element_type=jnp.float32).astype(jnp.bfloat16)
+            outs = [o_win[b, :, cols]] + [o_ent[i, :, cols] for i in range(7, ENTRIES)]
+            logs = [e_win[b, :, cols]] + [
+                jnp.where(at_b, e_ent[i, :, cols], -jnp.inf) for i, at_b in zip(range(7, ENTRIES), here)
+            ]
+            out, total, _ = merge(outs, logs)
+            att[pl.ds(b * BLOCK, BLOCK), cols] = (out / total).astype(jnp.bfloat16)
+    part = w_ref.shape[1] // 4
+    for n in range(4):
+        cols = pl.ds(n * part, part)
+        out_ref[:, cols] = jnp.dot(att[...], w_ref[:, cols], preferred_element_type=jnp.float32).astype(jnp.bfloat16)
     for kv in range(2):
         for twin in range(2):
             send_sel(0, twin, kv).wait_send()
@@ -548,7 +576,7 @@
     scalars = pl.BlockSpec(memory_space=pltpu.SMEM)
     out = pl.pallas_call(
         kernel,
-        out_shape=pltpu.VMEM((BLK_DEV, BLOCK, depth), bf16),
+        out_shape=pltpu.VMEM((BLK_DEV * BLOCK, depth), bf16),
         in_specs=[scalars, scalars, in_hbm, in_hbm, in_hbm],
         out_specs=pl.BlockSpec(memory_space=pltpu.VMEM),
         scratch_shapes=[
@@ -565,6 +593,7 @@
             vmem((PLANE, SLICE, width), bf16),
             vmem((RING, SLICE, 128), bf16),
             vmem((SLICE, width), bf16),
+            vmem((SLICE, 128), bf16),
             vmem((SLICE, width), bf16),
             vmem((GLOB, 2, BLOCK, width), bf16),
             vmem((BLK_DEV, BLOCK, width), bf16),
@@ -573,7 +602,7 @@
             vmem((ENTRIES, BLOCK, width), f32),
             vmem((BLK_DEV, BLOCK, width), f32),
             vmem((BLK_DEV, BLOCK, width), f32),
-            vmem((BLK_DEV, BLOCK, width), bf16),
+            vmem((BLK_DEV * BLOCK, width), bf16),
             table, table, table, table,
             pltpu.SMEM((ENTRIES,), jnp.int32),
             pltpu.SMEM((ENTRIES,), jnp.int32),
@@ -603,7 +632,7 @@
         keys_values.reshape(2, BLK_DEV, BLOCK, width),
         out_weight,
     )
-    return put(out.reshape(BLK_DEV * BLOCK, depth))
+    return put(out)
 
 
 def solution(mesh):

time: 132 us -> 128 us (0.970); the launches traced: 130 us -> 128 us
  Pallas kernels: 130 us -> 128 us
    pallas_call x1, Pallas kernels: 129 us -> 126 us  [local(): pl.pallas_call(kernel, out_shape=pltpu.VMEM((BLK_DEV * BLOCK, depth), bf1...]
where the time goes in v5:
time: 128 us
  Pallas kernels  128 us (100%)
    pallas_call x1, Pallas kernels, local(): pl.pallas_call(kernel, out_shape=pltpu.VMEM((BLK_DEV * BLOCK, depth), bf1...  126 us

profile of v5, /device:TPU:1, one launch (start us, length us, event | category | flops | bytes accessed | tf_op | source)
XLA Modules:
  0.0 127.5 jit_solution(9335593341516540811)
XLA Ops:
  0.0 126.4 %sparse_attention.1.x_ref = bf16[384,2048]{1,0:T(8,128)(2,1)S(1)} custom-call(s32[3,3]{1,0:T(4,128)} %rand_ref.1, s32[2]{0:T(128)} %ids_ref.1, bf16[3,128,1024]{2,1,0:T(8,128)(2,1)} %bitcast.3, bf16[2,3,128,1024]{3,2,1,0:T(8,128)(2,1)} %bitcast.2, bf16[1024,2048]{1,0:T(8,128)(2,1)} %w_hbm.1), custom_call_target="tpu_custom_call" | custom-call | tf_op jit(solution)/shard_map/sparse_attention/pallas_call | solution.py:577
  126.4 1.2 put.1

commit v6 on v5

--- a/solution.py
+++ b/solution.py
@@ -436,10 +436,6 @@
     def _(i):
         entry(i, 0)
 
-    global_here()
-    for b in range(BLK_DEV):
-        window(b)
-
     source = hop(3 * go_short) * 2 + core
     picks = [wanted(table, source) for table in (tab_ls, tab_lo)]
     for q in range(BLK_DEV):
@@ -455,7 +451,12 @@
 
     for twin in range(2):
         send_sel(1, twin, 0).start()
-    for q in range(BLK_DEV, CHUNKS):
+    global_here()
+    window(0)
+    window(1)
+    arrive_long(3, BLK_DEV)
+    window(2)
+    for q in range(BLK_DEV + 1, CHUNKS):
         arrive_long(3, q)
     for twin in range(2):
         stage4[twin, 1] = l3v[picks[twin]]

time: 128 us -> 125 us (0.977)
  Pallas kernels: 128 us -> 125 us
    pallas_call x1, Pallas kernels: 126 us -> 124 us  [local(): pl.pallas_call(kernel, out_shape=pltpu.VMEM((BLK_DEV * BLOCK, depth), bf1...]
where the time goes in v6:
time: 125 us
  Pallas kernels  125 us (100%)
    pallas_call x1, Pallas kernels, local(): pl.pallas_call(kernel, out_shape=pltpu.VMEM((BLK_DEV * BLOCK, depth), bf1...  124 us

profile of v6, /device:TPU:1, one launch (start us, length us, event | category | flops | bytes accessed | tf_op | source)
XLA Modules:
  0.0 125.0 jit_solution(2954995789742221728)
XLA Ops:
  0.0 123.8 %sparse_attention.1.x_ref = bf16[384,2048]{1,0:T(8,128)(2,1)S(1)} custom-call(s32[3,3]{1,0:T(4,128)} %rand_ref.1, s32[2]{0:T(128)} %ids_ref.1, bf16[3,128,1024]{2,1,0:T(8,128)(2,1)} %bitcast.3, bf16[2,3,128,1024]{3,2,1,0:T(8,128)(2,1)} %bitcast.2, bf16[1024,2048]{1,0:T(8,128)(2,1)} %w_hbm.1), custom_call_target="tpu_custom_call" | custom-call | tf_op jit(solution)/shard_map/sparse_attention/pallas_call | solution.py:578
  123.8 1.2 put.1

commit v7 on v6

--- a/solution.py
+++ b/solution.py
@@ -225,26 +225,23 @@
 
         sel1[...] = recv1[owner // SEG_DEV * 2 + owner % 2]
 
-    def scatter_z():
-        @pl.loop(1, RING)
-        def _(i):
-            to = (z + i) % RING
-            remote(sel1.at[:, cols_of(to)], recv2.at[z], s2.at[to], r2.at[z], at(to, core)).start()
-
-        recv2[z] = sel1[:, cols_of(z)]
-
-    def choose_in_ring():
-        @pl.loop(1, RING)
-        def _(i):
-            src = (z + i) % RING
-            remote(recv2.at[src], recv2.at[src], s2.at[src], r2.at[src], other).wait_recv()
-
-        piece[...] = recv2[owner // 2 % RING]
-
     def along_x(step):
         return seg // 4 * 4 + (seg + step) % 4
 
-    slot = along_x(3) * 2 + core
+    def scatter_z():
+        @pl.loop(0, RING)
+        def _(to):
+            there = along_x(1) * SEG_DEV + to * 2 + core
+            remote(sel1.at[:, cols_of(to)], recv2.at[z], s2.at[to], r2.at[z], there).start()
+
+    def choose_in_ring():
+        @pl.loop(0, RING)
+        def _(src):
+            remote(recv2.at[src], recv2.at[src], s2.at[src], r2.at[src], other).wait_recv()
+
+        piece[...] = recv2[owner // 2 % RING]
+
+    slot = along_x(2) * 2 + core
 
     def gather_z():
         @pl.loop(0, RING)
@@ -508,14 +505,10 @@
         for kv in range(2):
             edge(kv, other).wait_send()
 
-    @pl.loop(1, RING)
-    def _(i):
-        to = (z + i) % RING
+    @pl.loop(0, RING)
+    def _(to):
         there = sel1.at[:, cols_of(to)]
         remote(there, there, s2.at[to], r2.at[to], other).wait_send()
-
-    @pl.loop(0, RING)
-    def _(to):
         remote(piece, piece, s3.at[to], r3.at[to], other).wait_send()
 
     load_w.wait()

time: 125 us -> 125 us (level)
  no operation moved by 1% of the time
where the time goes in v7:
time: 125 us
  Pallas kernels  125 us (100%)
    pallas_call x1, Pallas kernels, local(): pl.pallas_call(kernel, out_shape=pltpu.VMEM((BLK_DEV * BLOCK, depth), bf1...  124 us

profile of v7, /device:TPU:1, one launch (start us, length us, event | category | flops | bytes accessed | tf_op | source)
XLA Modules:
  0.0 125.0 jit_solution(14971583010194817624)
XLA Ops:
  0.0 123.8 %sparse_attention.1.x_ref = bf16[384,2048]{1,0:T(8,128)(2,1)S(1)} custom-call(s32[3,3]{1,0:T(4,128)} %rand_ref.1, s32[2]{0:T(128)} %ids_ref.1, bf16[3,128,1024]{2,1,0:T(8,128)(2,1)} %bitcast.3, bf16[2,3,128,1024]{3,2,1,0:T(8,128)(2,1)} %bitcast.2, bf16[1024,2048]{1,0:T(8,128)(2,1)} %w_hbm.1), custom_call_target="tpu_custom_call" | custom-call | tf_op jit(solution)/shard_map/sparse_attention/pallas_call | solution.py:571
  123.8 1.2 put.1
